TPU v7x, 32 devices: a whole 2x2x4 slice. The times are simulated.
32 devices in a mesh: ctx: 8 (over z, core), fsdp: 4 (over y, x).
Axes of the slice: x: 2, y: 2, z: 4, core: 2. Of those that a mesh axis runs over, the one named last changes fastest.
Arguments:
- hidden_in: bfloat16 [4, 2048, 2048], P('fsdp', 'ctx'), may hold values from -6 to 6
- weight_query: bfloat16 [2048, 2048], P('fsdp'), may hold values from -0.125 to 0.125
- key_weight_matrix: bfloat16 [2048, 1024], P('fsdp'), may hold values from -0.125 to 0.125
- weight_value: bfloat16 [2048, 1024], P('fsdp'), may hold values from -0.125 to 0.125
- weight_out: bfloat16 [2048, 2048], P(None, 'fsdp'), may hold values from -0.5 to 0.5
- weight_gate: bfloat16 [2048, 6144], P('fsdp'), may hold values from -0.125 to 0.125
- weight_up: bfloat16 [2048, 6144], P('fsdp'), may hold values from -0.125 to 0.125
- weight_down: bfloat16 [6144, 2048], P(None, 'fsdp'), may hold values from -0.078125 to 0.078125
- gain_attention: bfloat16 [2048], P('fsdp'), may hold values from 0.5 to 1.5
- gain_feed: bfloat16 [2048], P('fsdp'), may hold values from 0.5 to 1.5
- gain_query: bfloat16 [128], P('fsdp'), may hold values from 0.25 to 1.75
- gain_key: bfloat16 [128], P('fsdp'), may hold values from 0.25 to 1.75
- positions: int32 [4, 2048], P('fsdp', 'ctx'), may hold values from 0 to 4095
- token_block_index: int32 [4, 2048], P('fsdp', 'ctx'), may hold values from 0 to 15, never falling along the last dimension, each value on 1 to 256 neighbouring positions
- grad_out: bfloat16 [4, 2048, 2048], P('fsdp', 'ctx'), may hold values from -6 to 6
Outputs:
- hidden_out: bfloat16 [4, 2048, 2048], P('fsdp', 'ctx')
- grad_hidden: float32 [4, 2048, 2048], P('fsdp', 'ctx')
- grad_weight_query: float32 [2048, 2048], P('fsdp')
- grad_weight_key: float32 [2048, 1024], P('fsdp')
- grad_weight_value: float32 [2048, 1024], P('fsdp')
- grad_weight_out: float32 [2048, 2048], P(None, 'fsdp')
- grad_weight_gate: float32 [2048, 6144], P('fsdp')
- grad_weight_up: float32 [2048, 6144], P('fsdp')
- grad_weight_down: float32 [6144, 2048], P(None, 'fsdp')
- grad_gain_attention: float32 [2048], P('fsdp')
- grad_gain_feed: float32 [2048], P('fsdp')
- grad_gain_query: float32 [128], P('fsdp')
- grad_gain_key: float32 [128], P('fsdp')
Inputs may be any that keep to these rules, and one draw needn't show every extreme that they name: `token_block_index`: within each sequence the block ids never fall; each block holds 1 to 256 consecutive tokens and one holds exactly 256.
All inputs are finite; a program needn't handle non-finite values.
Results may differ from a plain program's by a relative error of at most 0.025.
Values may be sent and summed in bfloat16 or wider, within the bound.
A program may use at most 640 MiB of HBM per device.

v0:
```python
import jax
import jax.numpy as jnp
from jax import lax
from jax.sharding import PartitionSpec as P

D = 2048
QUERY_HEADS = 16
KEY_VALUE_HEADS = 8
HEAD_SIZE = 128
FF = 6144
EPS = 1e-06
THETA = 1000000.0
NEGATIVE_LARGE = -1e30


def from_behind(shard, axis, by):
    peers = lax.axis_size(axis)
    return lax.ppermute(shard, axis, [(i, (i + by) % peers) for i in range(peers)])


def tdot(left, right):
    return lax.dot_general(
        left, right, (((0,), (0,)), ((), ())), preferred_element_type=jnp.float32
    )


def rdot(left, right):
    return lax.dot_general(
        left, right, (((1,), (1,)), ((), ())), preferred_element_type=jnp.float32
    )


def tables(positions):
    half = HEAD_SIZE // 2
    freq = THETA ** (-(jnp.arange(half).astype(jnp.float32) * 2.0 / HEAD_SIZE))
    angle = positions.astype(jnp.float32)[..., None] * freq
    return (jnp.cos(angle), jnp.sin(angle))


def rotary(value, cosine_table, sine_table):
    half = value.shape[-1] // 2
    first = value[..., :half]
    second = value[..., half:]
    return jnp.concatenate(
        [first * cosine_table - second * sine_table, second * cosine_table + first * sine_table],
        axis=-1,
    )


def reverse_rotation(grad, cosine_table, sine_table):
    half = grad.shape[-1] // 2
    first = grad[..., :half]
    second = grad[..., half:]
    return jnp.concatenate(
        [first * cosine_table + second * sine_table, second * cosine_table - first * sine_table],
        axis=-1,
    )


def rms_forward(value, gain):
    inverse = lax.rsqrt(jnp.mean(value * value, axis=-1, keepdims=True) + EPS)
    return (value * inverse * gain, inverse)


def rms_backward(value, inverse, gain, grad):
    scaled = grad * gain
    inner = jnp.mean(scaled * value, axis=-1, keepdims=True)
    return (inverse * scaled - value * inverse * inverse * inverse * inner, grad * value * inverse)


def local(
    hidden_in,
    weight_query,
    key_weight_matrix,
    weight_value,
    weight_out,
    weight_gate,
    weight_up,
    weight_down,
    gain_attention,
    gain_feed,
    gain_query,
    gain_key,
    positions,
    token_block_index,
    grad_out,
):
    gathered = (
        lax.all_gather(weight_query, "fsdp", axis=0, tiled=True),
        lax.all_gather(key_weight_matrix, "fsdp", axis=0, tiled=True),
        lax.all_gather(weight_value, "fsdp", axis=0, tiled=True),
        lax.all_gather(weight_out, "fsdp", axis=1, tiled=True),
        lax.all_gather(weight_gate, "fsdp", axis=0, tiled=True),
        lax.all_gather(weight_up, "fsdp", axis=0, tiled=True),
        lax.all_gather(weight_down, "fsdp", axis=1, tiled=True),
        lax.all_gather(gain_attention, "fsdp", axis=0, tiled=True),
        lax.all_gather(gain_feed, "fsdp", axis=0, tiled=True),
        lax.all_gather(gain_query, "fsdp", axis=0, tiled=True),
        lax.all_gather(gain_key, "fsdp", axis=0, tiled=True),
    )
    full_query, full_key, full_value, full_out, full_gate, full_up, full_down = gathered[:7]
    norm_attention = gathered[7].astype(jnp.float32)
    norm_feed = gathered[8].astype(jnp.float32)
    norm_query = gathered[9].astype(jnp.float32)
    norm_key = gathered[10].astype(jnp.float32)
    residual = hidden_in.reshape(-1, D).astype(jnp.float32)
    local_row_count = residual.shape[0]
    query_group = QUERY_HEADS // KEY_VALUE_HEADS
    scale = HEAD_SIZE ** (-0.5)
    key_total_width = KEY_VALUE_HEADS * HEAD_SIZE
    cosine_table, sine_table = tables(positions.reshape(-1))
    cosine_table = cosine_table[:, None, :]
    sine_table = sine_table[:, None, :]
    query_ids = token_block_index.reshape(-1)
    key_ids = lax.all_gather(token_block_index, "ctx", axis=1, tiled=True).reshape(-1)
    normed, inverse_one = rms_forward(residual, norm_attention)
    normed_low = normed.astype(jnp.bfloat16)
    query_proj = jnp.dot(normed_low, full_query, preferred_element_type=jnp.float32).reshape(
        local_row_count, QUERY_HEADS, HEAD_SIZE
    )
    query_normed, inverse_query = rms_forward(query_proj, norm_query)
    query_matrix = (
        (rotary(query_normed, cosine_table, sine_table) * scale)
        .astype(jnp.bfloat16)
        .reshape(local_row_count, KEY_VALUE_HEADS, query_group, HEAD_SIZE)
    )
    key_projected = jnp.dot(normed_low, full_key, preferred_element_type=jnp.float32).reshape(
        local_row_count, KEY_VALUE_HEADS, HEAD_SIZE
    )
    key_normed, inverse_key = rms_forward(key_projected, norm_key)
    key_row_values = (
        rotary(key_normed, cosine_table, sine_table)
        .astype(jnp.bfloat16)
        .reshape(local_row_count, key_total_width)
    )
    value_row_values = jnp.dot(normed_low, full_value, preferred_element_type=jnp.float32).astype(
        jnp.bfloat16
    )
    portion_keys = lax.all_gather(key_row_values, "ctx", axis=0, tiled=True)
    portion_values = lax.all_gather(value_row_values, "ctx", axis=0, tiled=True)
    token_count = portion_keys.shape[0]
    piece_ids = key_ids
    previous_maximum = jnp.full(
        (local_row_count, KEY_VALUE_HEADS, query_group), NEGATIVE_LARGE, jnp.float32
    )
    scores = jnp.einsum(
        "qgrd,kgd->qgrk",
        query_matrix,
        portion_keys.reshape(token_count, KEY_VALUE_HEADS, HEAD_SIZE),
        preferred_element_type=jnp.float32,
    )
    allowed = (piece_ids[None, :] <= query_ids[:, None])[:, None, None, :]
    masked = jnp.where(allowed, scores, NEGATIVE_LARGE)
    new_max = jnp.maximum(previous_maximum, jnp.max(masked, axis=-1))
    weights = jnp.where(allowed, jnp.exp(masked - new_max[..., None]), 0.0)
    new_sum = jnp.sum(weights, axis=-1)
    new_acc = jnp.einsum(
        "qgrk,kgd->qgrd",
        weights.astype(jnp.bfloat16),
        portion_values.reshape(token_count, KEY_VALUE_HEADS, HEAD_SIZE),
        preferred_element_type=jnp.float32,
    )
    log_total = new_max + jnp.log(new_sum)
    context = (
        (new_acc / new_sum[..., None])
        .reshape(local_row_count, QUERY_HEADS * HEAD_SIZE)
        .astype(jnp.bfloat16)
    )
    middle = residual + jnp.dot(context, full_out, preferred_element_type=jnp.float32)
    normed_two, inverse_two = rms_forward(middle, norm_feed)
    normed_two_low = normed_two.astype(jnp.bfloat16)
    gate_proj = jnp.dot(normed_two_low, full_gate, preferred_element_type=jnp.float32)
    up_proj = jnp.dot(normed_two_low, full_up, preferred_element_type=jnp.float32)
    sigma = jax.nn.sigmoid(gate_proj)
    activation = (gate_proj * sigma * up_proj).astype(jnp.bfloat16)
    hidden_out = (
        middle + jnp.dot(activation, full_down, preferred_element_type=jnp.float32)
    ).astype(jnp.bfloat16)
    grad_low = grad_out.reshape(local_row_count, D)
    grad_act = rdot(grad_low, full_down)
    grad_gate = (grad_act * up_proj * sigma * (1.0 + gate_proj * (1.0 - sigma))).astype(
        jnp.bfloat16
    )
    grad_upward = (grad_act * gate_proj * sigma).astype(jnp.bfloat16)
    fsdp_count = lax.axis_size("fsdp")
    shard_rows = D // fsdp_count
    select = lambda array: array
    picked = select(normed_two_low)
    feed_shard = lax.psum_scatter(
        jnp.concatenate(
            [
                tdot(picked, grad_gate),
                tdot(picked, grad_upward),
                tdot(select(grad_low), activation),
            ],
            axis=1,
        ).astype(jnp.bfloat16),
        "fsdp",
        scatter_dimension=0,
        tiled=True,
    ).astype(jnp.float32)
    grad_normed_two = rdot(grad_gate, full_gate) + rdot(grad_upward, full_up)
    back_two, gain_two_terms = rms_backward(middle, inverse_two, norm_feed, grad_normed_two)
    grad_middle = grad_low.astype(jnp.float32) + back_two
    grad_attention = grad_middle.astype(jnp.bfloat16)
    context_gradient = rdot(grad_attention, full_out).astype(jnp.bfloat16)
    context_head_gradient = context_gradient.reshape(
        local_row_count, KEY_VALUE_HEADS, query_group, HEAD_SIZE
    )
    delta = jnp.sum(
        (context_gradient.astype(jnp.float32) * context.astype(jnp.float32)).reshape(
            local_row_count, KEY_VALUE_HEADS, query_group, HEAD_SIZE
        ),
        axis=-1,
    )
    own_index = lax.axis_index("ctx")
    cycle_size = lax.axis_size("ctx")

    def cycle_step(step_index, state):
        rotating_keys, rotating_values, key_gradient, grad_values, grad_queries = state
        source = (own_index - step_index) % cycle_size
        piece_ids = lax.dynamic_slice_in_dim(key_ids, source * local_row_count, local_row_count)
        acc_keys = key_gradient
        acc_values = grad_values
        acc_queries = grad_queries
        key_head_rows = rotating_keys.reshape(local_row_count, KEY_VALUE_HEADS, HEAD_SIZE)
        value_head_rows = rotating_values.reshape(local_row_count, KEY_VALUE_HEADS, HEAD_SIZE)
        scores = jnp.einsum(
            "qgrd,kgd->qgrk", query_matrix, key_head_rows, preferred_element_type=jnp.float32
        )
        allowed = (piece_ids[None, :] <= query_ids[:, None])[:, None, None, :]
        probs = jnp.where(
            allowed, jnp.exp(jnp.where(allowed, scores, NEGATIVE_LARGE) - log_total[..., None]), 0.0
        )
        grad_probs = jnp.einsum(
            "qgrd,kgd->qgrk",
            context_head_gradient,
            value_head_rows,
            preferred_element_type=jnp.float32,
        )
        grad_scores = (probs * (grad_probs - delta[..., None])).astype(jnp.bfloat16)
        acc_values = acc_values + jnp.einsum(
            "qgrk,qgrd->kgd",
            probs.astype(jnp.bfloat16),
            context_head_gradient,
            preferred_element_type=jnp.float32,
        ).reshape(local_row_count, key_total_width)
        acc_keys = acc_keys + jnp.einsum(
            "qgrk,qgrd->kgd", grad_scores, query_matrix, preferred_element_type=jnp.float32
        ).reshape(local_row_count, key_total_width)
        acc_queries = acc_queries + jnp.einsum(
            "qgrk,kgd->qgrd", grad_scores, key_head_rows, preferred_element_type=jnp.float32
        )
        rotating_keys, rotating_values = from_behind((rotating_keys, rotating_values), "ctx", 1)
        key_gradient, grad_values = (
            from_behind(acc_keys.astype(jnp.bfloat16), "ctx", 1).astype(jnp.float32),
            from_behind(acc_values.astype(jnp.bfloat16), "ctx", 1).astype(jnp.float32),
        )
        return (rotating_keys, rotating_values, key_gradient, grad_values, acc_queries)

    cycle_start = (
        key_row_values,
        value_row_values,
        jnp.zeros((local_row_count, key_total_width), jnp.float32),
        jnp.zeros((local_row_count, key_total_width), jnp.float32),
        jnp.zeros((local_row_count, KEY_VALUE_HEADS, query_group, HEAD_SIZE), jnp.float32),
    )
    cycle_final = lax.fori_loop(0, cycle_size, cycle_step, cycle_start)
    key_gradient, grad_values, grad_queries = (cycle_final[2], cycle_final[3], cycle_final[4])
    query_back = reverse_rotation(
        grad_queries.reshape(local_row_count, QUERY_HEADS, HEAD_SIZE) * scale,
        cosine_table,
        sine_table,
    )
    back_query, query_gain_terms = rms_backward(query_proj, inverse_query, norm_query, query_back)
    grad_query_low = back_query.reshape(local_row_count, QUERY_HEADS * HEAD_SIZE).astype(
        jnp.bfloat16
    )
    key_backward = reverse_rotation(
        key_gradient.reshape(local_row_count, KEY_VALUE_HEADS, HEAD_SIZE), cosine_table, sine_table
    )
    back_key, key_gain_terms = rms_backward(key_projected, inverse_key, norm_key, key_backward)
    grad_key_low = back_key.reshape(local_row_count, key_total_width).astype(jnp.bfloat16)
    grad_value_low = grad_values.astype(jnp.bfloat16)
    grad_normed_one = (
        rdot(grad_query_low, full_query)
        + rdot(grad_key_low, full_key)
        + rdot(grad_value_low, full_value)
    )
    back_one, gain_one_terms = rms_backward(residual, inverse_one, norm_attention, grad_normed_one)
    grad_hidden = (grad_middle + back_one).reshape(hidden_in.shape)
    select = lambda array: array
    picked = select(normed_low)
    attention_shard = lax.psum_scatter(
        jnp.concatenate(
            [
                tdot(picked, grad_query_low),
                tdot(picked, grad_key_low),
                tdot(picked, grad_value_low),
                tdot(select(grad_attention), context),
            ],
            axis=1,
        ).astype(jnp.bfloat16),
        "fsdp",
        scatter_dimension=0,
        tiled=True,
    ).astype(jnp.float32)
    attention_shard, feed_shard = (
        lax.psum(attention_shard.astype(jnp.bfloat16), "ctx").astype(jnp.float32),
        lax.psum(feed_shard.astype(jnp.bfloat16), "ctx").astype(jnp.float32),
    )
    gain_totals = lax.psum(
        (
            jnp.sum(gain_one_terms, axis=0),
            jnp.sum(gain_two_terms, axis=0),
            jnp.sum(query_gain_terms, axis=(0, 1)),
            jnp.sum(key_gain_terms, axis=(0, 1)),
        ),
        ("ctx", "fsdp"),
    )
    fsdp_index = lax.axis_index("fsdp")
    head_rows = HEAD_SIZE // fsdp_count
    query_width = QUERY_HEADS * HEAD_SIZE
    grad_gain_attention = lax.dynamic_slice_in_dim(
        gain_totals[0], fsdp_index * shard_rows, shard_rows
    )
    grad_gain_feed = lax.dynamic_slice_in_dim(gain_totals[1], fsdp_index * shard_rows, shard_rows)
    grad_gain_query = lax.dynamic_slice_in_dim(gain_totals[2], fsdp_index * head_rows, head_rows)
    grad_gain_key = lax.dynamic_slice_in_dim(gain_totals[3], fsdp_index * head_rows, head_rows)
    grad_weight_query = attention_shard[:, :query_width]
    grad_weight_key = attention_shard[:, query_width : query_width + key_total_width]
    grad_weight_value = attention_shard[
        :, query_width + key_total_width : query_width + 2 * key_total_width
    ]
    grad_weight_out = attention_shard[:, query_width + 2 * key_total_width :].T
    grad_weight_gate = feed_shard[:, :FF]
    grad_weight_up = feed_shard[:, FF : 2 * FF]
    grad_weight_down = feed_shard[:, 2 * FF :].T
    return (
        hidden_out.reshape(hidden_in.shape),
        grad_hidden,
        grad_weight_query,
        grad_weight_key,
        grad_weight_value,
        grad_weight_out,
        grad_weight_gate,
        grad_weight_up,
        grad_weight_down,
        grad_gain_attention,
        grad_gain_feed,
        grad_gain_query,
        grad_gain_key,
    )


def solution(mesh):
    return jax.shard_map(
        local,
        mesh=mesh,
        in_specs=(
            P("fsdp", "ctx", None),
            P("fsdp", None),
            P("fsdp", None),
            P("fsdp", None),
            P(None, "fsdp"),
            P("fsdp", None),
            P("fsdp", None),
            P(None, "fsdp"),
            P("fsdp"),
            P("fsdp"),
            P("fsdp"),
            P("fsdp"),
            P("fsdp", "ctx"),
            P("fsdp", "ctx"),
            P("fsdp", "ctx", None),
        ),
        out_specs=(
            P("fsdp", "ctx", None),
            P("fsdp", "ctx", None),
            P("fsdp", None),
            P("fsdp", None),
            P("fsdp", None),
            P(None, "fsdp"),
            P("fsdp", None),
            P("fsdp", None),
            P(None, "fsdp"),
            P("fsdp"),
            P("fsdp"),
            P("fsdp"),
            P("fsdp"),
        ),
        check_vma=False,
    )
```

profile of v0, /device:TPU:0, one launch (start us, length us, event | category | flops | bytes accessed | tf_op | source)
XLA Modules:
  0.0 2910.7 jit_solution(13086285690502229014)
XLA Ops:
  9.5 9.5 all-gather
  19.3 46.0 %all-gather.12.cloned.1.call-done = bf16[2048,1024]{1,0:T(8,128)(2,1)} async-done(((bf16[512,1024]{1,0:T(8,128)(2,1)}), bf16[2048,1024]{1,0:T(8,128)(2,1)}) %all-gather.12.cloned.1.call-update) | async-done | bytes 4194320 | tf_op jit(solution)/shard_map/all_gather | solution.py:91
  71.5 9.0 all-reduce.5
  80.9 39.0 %all-gather.16.cloned.1.call-done = bf16[2048,1024]{1,0:T(8,128)(2,1)} async-done(((bf16[512,1024]{1,0:T(8,128)(2,1)}), bf16[2048,1024]{1,0:T(8,128)(2,1)}) %all-gather.16.cloned.1.call-update) | async-done | bytes 4194320 | tf_op jit(solution)/shard_map/all_gather | solution.py:90
  119.9 6.4 copy.85
  135.3 7.8 all-gather.1
  143.1 12.2 all_gather.45
  156.8 52.6 %all-gather.20.cloned.1.call-done = bf16[2048,2048]{1,0:T(8,128)(2,1)} async-done(((bf16[512,2048]{1,0:T(8,128)(2,1)}), bf16[2048,2048]{1,0:T(8,128)(2,1)}) %all-gather.20.cloned.1.call-update) | async-done | bytes 8388624 | tf_op jit(solution)/shard_map/all_gather | solution.py:89
  209.5 12.3 copy.86
  221.7 5.9 multiply_reduce_fusion.5
  238.7 19.4 all-gather.14.cloned.1.call-done
  258.1 6.4 copy.117
  264.5 42.1 %all-gather.18.cloned.1.call-done = bf16[2048,1024]{0,1:T(8,128)(2,1)} async-done(((bf16[256,1024]{0,1:T(8,128)(2,1)}), bf16[2048,1024]{0,1:T(8,128)(2,1)}) %all-gather.18.cloned.1.call-update) | async-done | bytes 4194320 | tf_op jit(solution)/shard_map/all_gather | solution.py:139
  306.7 17.4 fusion.20
  324.1 14.3 fusion.21
  338.4 15.8 fusion.48
  355.6 38.4 %all-gather.22.cloned.1.call-done = bf16[2048,2048]{1,0:T(8,128)(2,1)} async-done(((bf16[2048,512]{1,0:T(8,128)(2,1)}), bf16[2048,2048]{1,0:T(8,128)(2,1)}) %all-gather.22.cloned.1.call-update) | async-done | bytes 8388624 | tf_op jit(solution)/shard_map/all_gather | solution.py:92
  394.1 6.2 multiply_reduce_fusion.4
  400.5 223.2 %all-gather.26.cloned.1.call-done = bf16[2048,6144]{1,0:T(8,128)(2,1)} async-done(((bf16[512,6144]{1,0:T(8,128)(2,1)}), bf16[2048,6144]{1,0:T(8,128)(2,1)}) %all-gather.26.cloned.1.call-update) | async-done | bytes 25165840 | tf_op jit(solution)/shard_map/all_gather | solution.py:94
  623.7 15.5 fusion.76
  639.2 214.1 %all-gather.24.cloned.1.call-done = bf16[2048,6144]{1,0:T(8,128)(2,1)} async-done(((bf16[512,6144]{1,0:T(8,128)(2,1)}), bf16[2048,6144]{1,0:T(8,128)(2,1)}) %all-gather.24.cloned.1.call-update) | async-done | bytes 25165840 | tf_op jit(solution)/shard_map/all_gather | solution.py:93
  853.3 15.5 fusion.75
  868.8 214.0 %all-gather.28.cloned.1.call-done = bf16[6144,2048]{1,0:T(8,128)(2,1)} async-done(((bf16[6144,512]{1,0:T(8,128)(2,1)}), bf16[6144,2048]{1,0:T(8,128)(2,1)}) %all-gather.28.cloned.1.call-update) | async-done | bytes 25165840 | tf_op jit(solution)/shard_map/all_gather | solution.py:95
  1082.8 20.6 multiply_convert_fusion
  1103.4 13.5 fusion.77
  1116.8 15.1 multiply_reduce_fusion.1
  1134.5 5.8 convolution_convert_fusion.2
  1146.4 5.0 reduce_sum.132
  1155.2 283.0 %while.24 = (s32[]{:T(128)}, bf16[256,1024]{1,0:T(8,128)(2,1)}, bf16[256,1024]{1,0:T(8,128)(2,1)}, f32[256,1024]{0,1:T(8,128)}, f32[256,1024]{0,1:T(8,128)S(1)},...) while((s32[]{:T(128)}, bf16[256,1024]{1,0:T(8,128)(2,1)}, ...), condition=%wide.region_9.10_spmd.clone, body=%wide.region_8.9_spmd.clone.sunk | while | flops 1355874304 | bytes 62640716 | solution.py:268
  1185.4 5.6 collective-permute-done.1
  1220.7 5.6 collective-permute-done.1
  1245.0 5.4 collective-permute-done.2
  1256.1 5.6 collective-permute-done.1
  1280.3 5.4 collective-permute-done.2
  1291.4 5.6 collective-permute-done.1
  1315.6 5.4 collective-permute-done.2
  1326.7 5.6 collective-permute-done.1
  1350.9 5.4 collective-permute-done.2
  1362.0 5.6 collective-permute-done.1
  1386.2 5.4 collective-permute-done.2
  1397.3 5.6 collective-permute-done.1
  1421.5 5.4 collective-permute-done.2
  1432.6 5.6 collective-permute-done.1
  1457.3 5.9 convolution_convert_fusion.3
  1463.1 18.0 pad_maximum_fusion.1
  1481.2 14.1 convert_bitcast_fusion
  1495.3 14.0 convolution_convert_fusion
  1509.2 14.3 convolution_convert_fusion.1
  1523.5 51.4 %pad_maximum_fusion = bf16[2048,18432]{1,0:T(8,128)(2,1)} fusion(bf16[2048,6144]{1,0:T(8,128)(2,1)} %convert_bitcast_fusion, bf16[2048,6144]{1,0:T(8,128)(2,1)} %convolution_convert_fusion, bf16[2048,6144]{1,0:T(8,128)(2,1)} %convolution_convert_fusion.1), kind=kLoop, calls=%fused_computation.25 | loop fusion | flops 226492416 | bytes 150994944 | tf_op jit(solution)/shard_map/concatenate | solution.py:190
  1575.3 125.1 %reduce-scatter.5.cloned.1.call-done = bf16[512,6144]{0,1:T(8,128)(2,1)} async-done(((bf16[2048,6144]{0,1:T(8,128)(2,1)}), bf16[512,6144]{0,1:T(8,128)(2,1)}) %reduce-scatter.5.cloned.1.call-update) | async-done | bytes 6291472 | tf_op jit(solution)/shard_map/reduce_scatter | solution.py:294
  1700.4 629.3 %reduce-scatter.7.cloned.1.call-done = bf16[512,18432]{1,0:T(8,128)(2,1)} async-done(((bf16[2048,18432]{1,0:T(8,128)(2,1)}), bf16[512,18432]{1,0:T(8,128)(2,1)}) %reduce-scatter.7.cloned.1.call-update) | async-done | bytes 18874384
  2329.7 6.2 fusion.78
  2342.0 40.7 %all-reduce.3 = (f32[2048]{0:T(1024)S(1)}, f32[2048]{0:T(1024)S(1)}, f32[128]{0:T(128)S(1)}, f32[128]{0:T(128)S(1)}) all-reduce(f32[2048]{0:T(1024)S(1)} %get-tuple-element.451, f32[2048]{0:T(1024)S(1)} %copy-done.41, f32[128]{0:T(128)S(1)} %get-tuple-element.447, ...), channel_id=1, replica_groups=mesh['ctx'=8,'fsdp'=4] {'ctx','fsdp'}, use_global_device_ids=true, to_apply=%region_18.19 | all-reduce | flops 4352 | bytes 34816 | tf_op jit(solution)/shard_map/psum | solution.py:312
  2385.2 4.5 fusion.40
  2389.7 13.0 fusion.34
  2402.7 421.8 %all-reduce.8.cloned.1.call-done = (bf16[512,6144]{0,1:T(8,128)(2,1)}, bf16[512,18432]{1,0:T(8,128)(2,1)}) async-done(((bf16[512,6144]{0,1:T(8,128)(2,1)}, bf16[512,18432]{1,0:T(8,128)(2,1)}), (bf16[512,6144]{0,1:T(8,128)(2,1)}, bf16[512,18432]{1,0:T(8,128)(2,1)})) %all-reduce.8.cloned.1.call-update) | async-done | bytes 25165840 | tf_op jit(solution)/shard_map/psum | solution.py:309
  2824.5 4.5 slice.68
  2833.3 9.5 convert_element_type.226
  2842.8 9.6 fusion.72
  2852.4 13.0 convert_element_type.227
  2865.3 5.3 copy.99
  2875.5 4.6 slice_bitcast_fusion.1
  2880.2 10.6 slice_bitcast_fusion
  2890.8 12.6 copy.102
  (423 shorter events, 284.6 us)
Async XLA Ops:
  7.2 11.8 copy-start.4
  7.2 58.1 %all-gather.12.cloned.1.call-start = ((), (), s32[]{:S(2)}) async-start(), calls=%async_computation.2 | async-start | bytes 5242880 | tf_op jit(solution)/shard_map/all_gather | solution.py:91
  7.9 112.0 %all-gather.16.cloned.1.call-start = ((), (), s32[]{:S(2)}) async-start(), calls=%async_computation.4 | async-start | bytes 5242880 | tf_op jit(solution)/shard_map/all_gather | solution.py:90
  8.7 200.8 %all-gather.20.cloned.1.call-start = ((), (), s32[]{:S(2)}) async-start(), calls=%async_computation.6 | async-start | bytes 10485760 | tf_op jit(solution)/shard_map/all_gather | solution.py:89
  9.4 248.7 %all-gather.14.cloned.1.call-start = ((), (), s32[]{:S(2)}) async-start(), calls=%async_computation.3 | async-start | bytes 4718592 | tf_op jit(solution)/shard_map/all_gather | solution.py:140
  19.0 202.7 %copy-start.30 = (f32[4,1,512]{2,1,0:T(1,128)}, f32[4,1,512]{2,1,0:T(1,128)S(1)}, u32[]{:S(2)}) copy-start(f32[4,1,512]{2,1,0:T(1,128)S(1)} %convert_element_type.229) | copy-start | bytes 24580
  19.3 202.4 %copy-start.36 = (f32[256]{0:T(256)}, f32[256]{0:T(256)S(1)}, u32[]{:S(2)}) copy-start(f32[256]{0:T(256)S(1)} %add_rsqrt_fusion.3) | copy-start | bytes 3076
  65.3 15.2 copy-start.48
  69.7 237.0 %all-gather.18.cloned.1.call-start = ((), (), s32[]{:S(2)}) async-start(), calls=%async_computation.5 | async-start | bytes 4718592 | tf_op jit(solution)/shard_map/all_gather | solution.py:139
  80.5 49.6 %copy-start.42 = (f32[128]{0:T(128)}, f32[128]{0:T(128)S(1)}, u32[]{:S(2)}) copy-start(f32[128]{0:T(128)S(1)} %convert_element_type.200) | copy-start | bytes 1540
  80.9 147.2 %copy-start.24 = (f32[256,64]{0,1:T(8,128)}, f32[256,64]{0,1:T(8,128)S(1)}, u32[]{:S(2)}) copy-start(f32[256,64]{0,1:T(8,128)S(1)} %get-tuple-element.504) | copy-start | bytes 196612
  80.9 147.2 %copy-start.26 = (f32[256,64]{0,1:T(8,128)}, f32[256,64]{0,1:T(8,128)S(1)}, u32[]{:S(2)}) copy-start(f32[256,64]{0,1:T(8,128)S(1)} %get-tuple-element.505) | copy-start | bytes 196612
  132.3 261.8 %all-gather.22.cloned.1.call-start = ((), (), s32[]{:S(2)}) async-start(), calls=%async_computation.7 | async-start | bytes 10485760 | tf_op jit(solution)/shard_map/all_gather | solution.py:92
  132.9 490.8 %all-gather.26.cloned.1.call-start = ((), (), s32[]{:S(2)}) async-start(), calls=%async_computation.9 | async-start | bytes 31457280 | tf_op jit(solution)/shard_map/all_gather | solution.py:94
  133.6 719.7 %all-gather.24.cloned.1.call-start = ((), (), s32[]{:S(2)}) async-start(), calls=%async_computation.8 | async-start | bytes 31457280 | tf_op jit(solution)/shard_map/all_gather | solution.py:93
  134.4 21.4 copy-start.20
  134.4 948.4 %all-gather.28.cloned.1.call-start = ((), (), s32[]{:S(2)}) async-start(), calls=%async_computation.10 | async-start | bytes 31457280 | tf_op jit(solution)/shard_map/all_gather | solution.py:95
  135.2 1565.2 %reduce-scatter.5.cloned.1.call-start = ((), (), s32[]{:S(2)}) async-start(), calls=%async_computation.11 | async-start | bytes 31457280 | tf_op jit(solution)/shard_map/reduce_scatter | solution.py:294
  135.3 92.4 %copy-start.44 = (f32[128]{0:T(128)}, f32[128]{0:T(128)S(1)}, u32[]{:S(2)}) copy-start(f32[128]{0:T(128)S(1)} %convert_element_type.205) | copy-start | bytes 1540
  155.3 66.4 %copy-start.38 = (s32[1,2048]{1,0:T(1,128)}, s32[1,2048]{1,0:T(1,128)S(1)}, u32[]{:S(2)}) copy-start(s32[1,2048]{1,0:T(1,128)S(1)} %all_gather.45) | copy-start | bytes 24580
  400.2 731.7 %copy-start.8 = (f32[256,2048]{1,0:T(8,128)}, f32[256,2048]{1,0:T(8,128)S(1)}, u32[]{:S(2)}) copy-start(f32[256,2048]{1,0:T(8,128)S(1)} %get-tuple-element.513) | copy-start | bytes 6291460
  400.5 452.8 %copy-start.15 = (bf16[256,2048]{1,0:T(8,128)(2,1)}, bf16[256,2048]{1,0:T(8,128)(2,1)S(1)}, u32[]{:S(2)}) copy-start(bf16[256,2048]{1,0:T(8,128)(2,1)S(1)} %multiply_convert_fusion.3) | copy-start | bytes 3145732
  1116.8 15.1 copy-start.21
  1155.2 283.0 %copy-start.25 = (f32[256,64]{0,1:T(8,128)S(1)}, f32[256,64]{0,1:T(8,128)}, u32[]{:S(2)}) copy-start(f32[256,64]{0,1:T(8,128)} %copy-done.24) | copy-start | bytes 196612
  1155.2 283.0 %copy-start.27 = (f32[256,64]{0,1:T(8,128)S(1)}, f32[256,64]{0,1:T(8,128)}, u32[]{:S(2)}) copy-start(f32[256,64]{0,1:T(8,128)} %copy-done.26) | copy-start | bytes 196612
  1155.2 284.5 %copy-start.35 = (f32[256,8]{0,1:T(8,128)S(1)}, f32[256,8]{0,1:T(8,128)}, u32[]{:S(2)}) copy-start(f32[256,8]{0,1:T(8,128)} %copy-done.34) | copy-start | bytes 24580
  1155.2 284.5 %copy-start.43 = (f32[128]{0:T(128)S(1)}, f32[128]{0:T(128)}, u32[]{:S(2)}) copy-start(f32[128]{0:T(128)} %copy-done.42) | copy-start | bytes 1540
  1162.5 13.0 collective-permute-start.3
  1169.1 10.7 collective-permute-start.2
  1170.7 14.7 collective-permute-start
  1170.7 20.3 collective-permute-start.1
  1197.8 11.9 collective-permute-start.3
  1204.4 10.7 collective-permute-start.2
  1204.4 16.3 collective-permute-start
  1204.4 21.9 collective-permute-start.1
  1233.2 10.7 collective-permute-start.3
  1239.7 10.7 collective-permute-start.2
  1239.7 16.3 collective-permute-start
  1239.7 21.9 collective-permute-start.1
  1268.5 10.7 collective-permute-start.3
  1275.0 10.7 collective-permute-start.2
  1275.0 16.3 collective-permute-start
  1275.0 21.9 collective-permute-start.1
  1303.8 10.7 collective-permute-start.3
  1310.3 10.7 collective-permute-start.2
  1310.3 16.3 collective-permute-start
  1310.3 21.9 collective-permute-start.1
  1339.1 10.7 collective-permute-start.3
  1345.6 10.7 collective-permute-start.2
  1345.7 16.3 collective-permute-start
  1345.7 21.9 collective-permute-start.1
  1374.4 10.7 collective-permute-start.3
  1381.0 10.7 collective-permute-start.2
  1381.0 16.3 collective-permute-start
  1381.0 21.9 collective-permute-start.1
  1409.7 10.7 collective-permute-start.3
  1416.3 10.7 collective-permute-start.2
  1416.3 16.3 collective-permute-start
  1416.3 21.9 collective-permute-start.1
  1481.1 848.6 %reduce-scatter.7.cloned.1.call-start = ((), (), s32[]{:S(2)}) async-start(), calls=%async_computation.12 | async-start | bytes 94371840
  1575.0 1249.5 %all-reduce.8.cloned.1.call-start = ((), (), s32[]{:S(2)}) async-start(), calls=%async_computation.13 | async-start | bytes 50331648 | tf_op jit(solution)/shard_map/psum | solution.py:309
  2824.5 18.3 slice-start
  2824.5 18.3 slice-start.1
  2829.0 13.8 slice-start.2
  (60 other events, 202.6 us)
Sparse Core Ops, SparseCore 0:
  9.9 55.3 all-gather.11
  67.2 52.6 all-gather.15
  121.7 87.6 all-gather.19
  210.9 47.1 all-gather.13
  260.1 46.5 all-gather.17
  308.3 85.6 all-gather.21
  395.9 227.7 all-gather.25
  625.6 227.7 all-gather.23
  855.2 227.5 all-gather.27
  1481.2 219.1 reduce-scatter.4
  1703.8 625.8 reduce-scatter.6
  2332.2 492.2 all-reduce.7
where the time goes:
time: 2920 us; the launch traced here: 2910 us
  waiting for transfers between devices  2180 us (75%)
  matrix products  284 us (10%)
  other arithmetic  175 us (6%)
  local copies, waits for them, and re-layouts  165 us (6%)
  blocking collectives  79.3 us (3%)
    unnamed x13, waiting for transfers between devices  634 us
    psum x1, waiting for transfers between devices, local(): lax.psum(attention_shard.astype(jnp.bfloat16), 'ctx').astype(jnp.float32)  422 us
    all_gather x1, waiting for transfers between devices, local(): lax.all_gather(weight_up, 'fsdp', axis=0, tiled=True)  223 us
    all_gather x1, waiting for transfers between devices, local(): lax.all_gather(weight_gate, 'fsdp', axis=0, tiled=True)  214 us
    all_gather x1, waiting for transfers between devices, local(): lax.all_gather(weight_down, 'fsdp', axis=1, tiled=True)  214 us
    reduce_scatter x1, waiting for transfers between devices, local(): lax.psum_scatter(jnp.concatenate([tdot(picked, grad_query_low), tdot(pick...  125 us
    ppermute x32, waiting for transfers between devices, from_behind(): lax.ppermute(shard, axis, [(i, (i + by) % peers) for i in range(peers)])  114 us
    dot_general x7, matrix products, rdot(): lax.dot_general(left, right, (((1,), (1,)), ((), ())), preferred_element_...  63.1 us
  transfers between devices with their start and end apart: 44, of which 42 were waited for; matrix products, arithmetic and copies ran while one was open for 13% of the time, Pallas kernels for 0%

commit v1 on v0

--- a/solution.py
+++ b/solution.py
@@ -85,12 +85,27 @@
     token_block_index,
     grad_out,
 ):
+
+    def review_runs(u_in, named_axis):
+        amount_of = lax.psum(1, named_axis)
+        samples = tuple(((kk, (kk + 1) % amount_of) for kk in range(amount_of)))
+        stack_in = tuple(((kk, (kk - 1) % amount_of) for kk in range(amount_of)))
+        last, e_now = ([u_in], [u_in])
+        for _ in range(amount_of // 2):
+            last.append(lax.ppermute(last[-1], named_axis, samples))
+        for _ in tuple(range((amount_of - 1) // 2)):
+            e_now.append(lax.ppermute(e_now[-1], named_axis, stack_in))
+        latest = jnp.concatenate([*last[::-1], *e_now[1:]], axis=0)
+        return jnp.roll(
+            latest, shift=(lax.axis_index(named_axis) - amount_of // 2) * u_in.shape[0], axis=0
+        )
+
     gathered = (
         lax.all_gather(weight_query, "fsdp", axis=0, tiled=True),
         lax.all_gather(key_weight_matrix, "fsdp", axis=0, tiled=True),
         lax.all_gather(weight_value, "fsdp", axis=0, tiled=True),
         lax.all_gather(weight_out, "fsdp", axis=1, tiled=True),
-        lax.all_gather(weight_gate, "fsdp", axis=0, tiled=True),
+        review_runs(weight_gate, "fsdp"),
         lax.all_gather(weight_up, "fsdp", axis=0, tiled=True),
         lax.all_gather(weight_down, "fsdp", axis=1, tiled=True),
         lax.all_gather(gain_attention, "fsdp", axis=0, tiled=True),

time: 2920 us -> 3020 us (1.034)
  blocking collectives: 79.3 us -> 479 us
  waiting for transfers between devices: 2180 us -> 1800 us
  local copies, waits for them, and re-layouts: 165 us -> 218 us
    all_gather x1, blocking collectives: 7.83 us -> 407 us  [local(): lax.all_gather(gain_feed, 'fsdp', axis=0, tiled=True)]
    all_gather x1, waiting for transfers between devices: 223 us -> 0.02 us  [local(): lax.all_gather(weight_up, 'fsdp', axis=0, tiled=True)]
    all_gather x1 -> x0, waiting for transfers between devices: 214 us -> none  [local(): lax.all_gather(weight_gate, 'fsdp', axis=0, tiled=True)]
    ppermute x0 -> x3, waiting for transfers between devices: none -> 201 us  [the longest x2 201 us: review_runs(): last.append(lax.ppermute(last[-1], named_axis, samples))]
    all_gather x1, waiting for transfers between devices: 52.6 us -> 0.01 us  [local(): lax.all_gather(weight_query, 'fsdp', axis=0, tiled=True)]
    unnamed x127 -> x136, local copies, waits for them, and re-layouts: 33.5 us -> 76.9 us
    all_gather x1, waiting for transfers between devices: 42.1 us -> 0.01 us  [local(): portion_keys = lax.all_gather(key_row_values, 'ctx', axis=0, tiled=True)]
    all_gather x1, waiting for transfers between devices: 38.4 us -> 0.01 us  [local(): lax.all_gather(weight_out, 'fsdp', axis=1, tiled=True)]
  transfers between devices with their start and end apart: 44 -> 46, of which waited for: 42 -> 39; matrix products, arithmetic and copies ran while one was open for 13% -> 13% of each run, Pallas kernels for 0% -> 0%
where the time goes in v1:
time: 3020 us; the launch traced here: 3010 us
  waiting for transfers between devices  1800 us (60%)
  blocking collectives  479 us (16%)
  matrix products  297 us (10%)
  local copies, waits for them, and re-layouts  218 us (7%)
  other arithmetic  186 us (6%)
    unnamed x12, waiting for transfers between devices  633 us
    psum x1, waiting for transfers between devices, local(): lax.psum(attention_shard.astype(jnp.bfloat16), 'ctx').astype(jnp.float32)  420 us
    all_gather x1, blocking collectives, local(): lax.all_gather(gain_feed, 'fsdp', axis=0, tiled=True)  407 us
    all_gather x1, waiting for transfers between devices, local(): lax.all_gather(weight_down, 'fsdp', axis=1, tiled=True)  204 us
    ppermute x2, waiting for transfers between devices, review_runs(): last.append(lax.ppermute(last[-1], named_axis, samples))  201 us
    ppermute x32, waiting for transfers between devices, from_behind(): lax.ppermute(shard, axis, [(i, (i + by) % peers) for i in range(peers)])  134 us
    reduce_scatter x1, waiting for transfers between devices, local(): lax.psum_scatter(jnp.concatenate([tdot(picked, grad_query_low), tdot(pick...  124 us
    unnamed x136, local copies, waits for them, and re-layouts  76.9 us
  transfers between devices with their start and end apart: 46, of which 39 were waited for; matrix products, arithmetic and copies ran while one was open for 13% of the time, Pallas kernels for 0%

profile of v1, /device:TPU:0, one launch (start us, length us, event | category | flops | bytes accessed | tf_op | source)
XLA Modules:
  0.0 3006.2 jit_solution(16112701161821830357)
XLA Ops:
  9.5 9.5 all-gather
  19.4 45.9 %all-gather.11.cloned.1.call-done = bf16[2048,1024]{1,0:T(8,128)(2,1)} async-done(((bf16[512,1024]{1,0:T(8,128)(2,1)}), bf16[2048,1024]{1,0:T(8,128)(2,1)}) %all-gather.11.cloned.1.call-update) | async-done | bytes 4194320 | tf_op jit(solution)/shard_map/all_gather | solution.py:106
  65.3 4.3 convolution_convert_fusion.7
  71.5 9.0 all-reduce.5
  80.8 39.1 %all-gather.15.cloned.1.call-done = bf16[2048,1024]{1,0:T(8,128)(2,1)} async-done(((bf16[512,1024]{1,0:T(8,128)(2,1)}), bf16[2048,1024]{1,0:T(8,128)(2,1)}) %all-gather.15.cloned.1.call-update) | async-done | bytes 4194320 | tf_op jit(solution)/shard_map/all_gather | solution.py:105
  119.9 6.4 copy.85
  135.8 200.9 %collective-permute-done.4 = bf16[512,6144]{1,0:T(8,128)(2,1)} collective-permute-done((bf16[512,6144]{1,0:T(8,128)(2,1)}, bf16[512,6144]{1,0:T(8,128)(2,1)}, u32[]{:S(2)}, u32[]{:S(2)}) %collective-permute-start.4) | collective-permute-done | bytes 6291488 | tf_op jit(solution)/shard_map/ppermute | solution.py:95
  339.7 407.2 %all-gather.1 = bf16[4,1,512]{2,1,0:T(2,128)(2,1)S(1)} all-gather(bf16[1,1,512]{2,1,0:T(2,128)(2,1)S(1)} %reshape.361), channel_id=1, replica_groups=mesh['ctx'=8,'fsdp'=4] {'fsdp'}, dimensions={0}, use_global_device_ids=true | all-gather | bytes 5120 | tf_op jit(solution)/shard_map/all_gather | solution.py:112
  746.9 12.3 all_gather.42
  760.7 12.2 copy.86
  772.9 5.9 multiply_reduce_fusion.5
  789.7 6.3 constant_dynamic-update-slice_fusion.7
  796.0 6.4 constant_dynamic-update-slice_fusion.6
  805.4 6.2 constant_dynamic-update-slice_fusion.4
  811.6 6.2 constant_dynamic-update-slice_fusion.3
  817.8 6.3 constant_dynamic-update-slice_fusion.2
  827.1 6.2 constant_dynamic-update-slice_fusion
  833.3 6.4 copy.117
  839.7 15.6 fusion.20
  855.4 14.5 fusion.21
  869.9 15.1 fusion.55
  886.4 6.2 multiply_reduce_fusion.4
  892.9 19.6 fusion.84
  912.5 203.5 %all-gather.25.cloned.1.call-done = bf16[6144,2048]{1,0:T(8,128)(2,1)} async-done(((bf16[6144,512]{1,0:T(8,128)(2,1)}), bf16[6144,2048]{1,0:T(8,128)(2,1)}) %all-gather.25.cloned.1.call-update) | async-done | bytes 25165840 | tf_op jit(solution)/shard_map/all_gather | solution.py:110
  1116.1 13.8 fusion.59
  1129.8 22.1 multiply_convert_fusion.1
  1152.0 13.5 fusion.85
  1165.4 15.2 multiply_reduce_fusion.1
  1183.2 5.8 convolution_convert_fusion.2
  1203.1 328.4 %while.24 = (s32[]{:T(128)}, bf16[256,1024]{1,0:T(8,128)(2,1)}, bf16[256,1024]{1,0:T(8,128)(2,1)}, f32[256,1024]{0,1:T(8,128)}, f32[256,1024]{0,1:T(8,128)}, /*i...) while((s32[]{:T(128)}, bf16[256,1024]{1,0:T(8,128)(2,1)}, ...), condition=%wide.region_9.10_spmd.clone, body=%wide.region_8.9_spmd.clone.sunk | while | flops 1355874304 | bytes 68932240 | solution.py:283
  1238.7 5.6 collective-permute-done.1
  1279.8 5.6 collective-permute-done.1
  1305.0 4.6 collective-permute-done.2
  1320.8 5.6 collective-permute-done.1
  1346.0 4.6 collective-permute-done.2
  1361.8 5.6 collective-permute-done.1
  1387.0 4.6 collective-permute-done.2
  1402.8 5.6 collective-permute-done.1
  1428.0 4.6 collective-permute-done.2
  1443.8 5.6 collective-permute-done.1
  1469.0 4.6 collective-permute-done.2
  1484.9 5.6 collective-permute-done.1
  1510.1 4.6 collective-permute-done.2
  1525.9 5.6 collective-permute-done.1
  1541.5 5.9 convolution_convert_fusion.3
  1554.2 18.0 pad_maximum_fusion.1
  1572.3 14.3 convert_bitcast_fusion
  1586.6 14.3 convolution_convert_fusion
  1600.9 14.3 convolution_convert_fusion.1
  1615.2 52.5 %pad_maximum_fusion = bf16[2048,18432]{1,0:T(8,128)(2,1)} fusion(bf16[2048,6144]{1,0:T(8,128)(2,1)} %convert_bitcast_fusion, bf16[2048,6144]{1,0:T(8,128)(2,1)} %convolution_convert_fusion, bf16[2048,6144]{1,0:T(8,128)(2,1)} %convolution_convert_fusion.1), kind=kLoop, calls=%fused_computation.25 | loop fusion | flops 226492416 | bytes 150994944 | tf_op jit(solution)/shard_map/concatenate | solution.py:205
  1667.9 123.6 %reduce-scatter.5.cloned.1.call-done = bf16[512,6144]{0,1:T(8,128)(2,1)} async-done(((bf16[2048,6144]{0,1:T(8,128)(2,1)}), bf16[512,6144]{0,1:T(8,128)(2,1)}) %reduce-scatter.5.cloned.1.call-update) | async-done | bytes 6291472 | tf_op jit(solution)/shard_map/reduce_scatter | solution.py:309
  1791.5 629.2 %reduce-scatter.7.cloned.1.call-done = bf16[512,18432]{1,0:T(8,128)(2,1)} async-done(((bf16[2048,18432]{1,0:T(8,128)(2,1)}), bf16[512,18432]{1,0:T(8,128)(2,1)}) %reduce-scatter.7.cloned.1.call-update) | async-done | bytes 18874384
  2421.9 5.9 fusion.86
  2434.2 41.1 %all-reduce.3 = (f32[2048]{0:T(1024)S(1)}, f32[2048]{0:T(1024)S(1)}, f32[128]{0:T(128)S(1)}, f32[128]{0:T(128)S(1)}) all-reduce(f32[2048]{0:T(1024)S(1)} %get-tuple-element.451, f32[2048]{0:T(1024)S(1)} %copy-done.47, f32[128]{0:T(128)S(1)} %get-tuple-element.447, ...), channel_id=1, replica_groups=mesh['ctx'=8,'fsdp'=4] {'ctx','fsdp'}, use_global_device_ids=true, to_apply=%region_18.19 | all-reduce | flops 4352 | bytes 34816 | tf_op jit(solution)/shard_map/psum | solution.py:327
  2477.8 4.2 fusion.47
  2482.0 13.7 fusion.41
  2495.7 419.9 %all-reduce.8.cloned.1.call-done = (bf16[512,6144]{0,1:T(8,128)(2,1)}, bf16[512,18432]{1,0:T(8,128)(2,1)}) async-done(((bf16[512,6144]{0,1:T(8,128)(2,1)}, bf16[512,18432]{1,0:T(8,128)(2,1)}), (bf16[512,6144]{0,1:T(8,128)(2,1)}, bf16[512,18432]{1,0:T(8,128)(2,1)})) %all-reduce.8.cloned.1.call-update) | async-done | bytes 25165840 | tf_op jit(solution)/shard_map/psum | solution.py:324
  2915.6 21.3 convert_element_type.227
  2941.1 9.7 fusion.81
  2950.7 6.4 convert_element_type.226
  2961.6 10.6 slice_bitcast_fusion
  2972.2 12.6 copy.102
  2984.8 4.6 slice_bitcast_fusion.1
  2989.4 5.3 copy.99
  (468 shorter events, 348.3 us)
Async XLA Ops:
  7.2 58.1 %all-gather.11.cloned.1.call-start = ((), (), s32[]{:S(2)}) async-start(), calls=%async_computation.2 | async-start | bytes 5242880 | tf_op jit(solution)/shard_map/all_gather | solution.py:106
  7.9 112.0 %all-gather.15.cloned.1.call-start = ((), (), s32[]{:S(2)}) async-start(), calls=%async_computation.4 | async-start | bytes 5242880 | tf_op jit(solution)/shard_map/all_gather | solution.py:105
  8.7 752.0 %all-gather.19.cloned.1.call-start = ((), (), s32[]{:S(2)}) async-start(), calls=%async_computation.6 | async-start | bytes 10485760 | tf_op jit(solution)/shard_map/all_gather | solution.py:104
  9.4 823.9 %all-gather.13.cloned.1.call-start = ((), (), s32[]{:S(2)}) async-start(), calls=%async_computation.3 | async-start | bytes 4718592 | tf_op jit(solution)/shard_map/all_gather | solution.py:155
  19.0 753.9 %copy-start.36 = (f32[4,1,512]{2,1,0:T(1,128)}, f32[4,1,512]{2,1,0:T(1,128)S(1)}, u32[]{:S(2)}) copy-start(f32[4,1,512]{2,1,0:T(1,128)S(1)} %convert_element_type.229) | copy-start | bytes 24580
  19.3 50.4 %copy-start.54 = (s32[1,256]{1,0:T(1,128)S(1)}, s32[1,256]{1,0:T(1,128)}, u32[]{:S(2)}) copy-start(s32[1,256]{1,0:T(1,128)} %param.29) | copy-start | bytes 3076
  19.3 50.4 %copy-start.57 = (u32[32]{0:T(128)S(1)}, u32[32]{0:T(128)}, u32[]{:S(2)}) copy-start(u32[32]{0:T(128)} %constant.164) | copy-start | bytes 388
  19.3 51.6 %copy-start.55 = (bf16[32]{0:T(256)(128)(2,1)S(1)}, bf16[32]{0:T(256)(128)(2,1)}, u32[]{:S(2)}) copy-start(bf16[32]{0:T(256)(128)(2,1)} %param.28) | copy-start | bytes 196
  19.4 51.9 %copy-start.56 = (bf16[32]{0:T(256)(128)(2,1)S(1)}, bf16[32]{0:T(256)(128)(2,1)}, u32[]{:S(2)}) copy-start(bf16[32]{0:T(256)(128)(2,1)} %param.27) | copy-start | bytes 196
  19.4 753.5 %copy-start.42 = (f32[256]{0:T(256)}, f32[256]{0:T(256)S(1)}, u32[]{:S(2)}) copy-start(f32[256]{0:T(256)S(1)} %add_rsqrt_fusion.3) | copy-start | bytes 3076
  69.6 770.1 %all-gather.17.cloned.1.call-start = ((), (), s32[]{:S(2)}) async-start(), calls=%async_computation.5 | async-start | bytes 4718592 | tf_op jit(solution)/shard_map/all_gather | solution.py:154
  80.8 698.4 %copy-start.30 = (f32[256,64]{0,1:T(8,128)}, f32[256,64]{0,1:T(8,128)S(1)}, u32[]{:S(2)}) copy-start(f32[256,64]{0,1:T(8,128)S(1)} %get-tuple-element.504) | copy-start | bytes 196612
  80.8 698.4 %copy-start.32 = (f32[256,64]{0,1:T(8,128)}, f32[256,64]{0,1:T(8,128)S(1)}, u32[]{:S(2)}) copy-start(f32[256,64]{0,1:T(8,128)S(1)} %get-tuple-element.505) | copy-start | bytes 196612
  132.3 754.1 %all-gather.21.cloned.1.call-start = ((), (), s32[]{:S(2)}) async-start(), calls=%async_computation.7 | async-start | bytes 10485760 | tf_op jit(solution)/shard_map/all_gather | solution.py:107
  132.9 760.0 %all-gather.23.cloned.1.call-start = ((), (), s32[]{:S(2)}) async-start(), calls=%async_computation.8 | async-start | bytes 31457280 | tf_op jit(solution)/shard_map/all_gather | solution.py:109
  133.7 206.0 %copy-start.53 = (bf16[512]{0:T(512)(128)(2,1)S(1)}, bf16[512]{0:T(512)(128)(2,1)}, u32[]{:S(2)}) copy-start(bf16[512]{0:T(512)(128)(2,1)} %param.26) | copy-start | bytes 3076
  133.7 613.3 %copy-start.45 = (s32[1,256]{1,0:T(1,128)S(1)}, s32[1,256]{1,0:T(1,128)}, u32[]{:S(2)}) copy-start(s32[1,256]{1,0:T(1,128)} %param.30) | copy-start | bytes 3076
  133.7 626.0 %copy-start.26 = (bf16[256,8,128]{0,2,1:T(8,128)(2,1)S(1)}, bf16[256,8,128]{0,2,1:T(8,128)(2,1)}, u32[]{:S(2)}) copy-start(bf16[256,8,128]{0,2,1:T(8,128)(2,1)} %pad_maximum_fusion.4) | copy-start | bytes 1572868
  133.7 982.4 %all-gather.25.cloned.1.call-start = ((), (), s32[]{:S(2)}) async-start(), calls=%async_computation.9 | async-start | bytes 31457280 | tf_op jit(solution)/shard_map/all_gather | solution.py:110
  134.4 1657.0 %reduce-scatter.5.cloned.1.call-start = ((), (), s32[]{:S(2)}) async-start(), calls=%async_computation.10 | async-start | bytes 31457280 | tf_op jit(solution)/shard_map/reduce_scatter | solution.py:309
  134.5 202.3 %collective-permute-start.4 = (bf16[512,6144]{1,0:T(8,128)(2,1)}, bf16[512,6144]{1,0:T(8,128)(2,1)}, u32[]{:S(2)}, u32[]{:S(2)}) collective-permute-start(bf16[512,6144]{1,0:T(8,128)(2,1)} %param.22), channel_id=1, source_target_pairs={{0,1},{1,2},{2,3},{3,0},{4,5},{5,6},{6,7},{7,4},{8,9},{9,10},{10,1... | collective-permute-start | bytes 18874376 | tf_op jit(solution)/shard_map/ppermute | solution.py:95
  336.8 453.0 %collective-permute-start.5 = (bf16[512,6144]{1,0:T(8,128)(2,1)}, bf16[512,6144]{1,0:T(8,128)(2,1)}, u32[]{:S(2)}, u32[]{:S(2)}) collective-permute-start(bf16[512,6144]{1,0:T(8,128)(2,1)} %collective-permute-done.4), channel_id=1, source_target_pairs={{0,1},{1,2},{2,3},{3,0},{4,5},{5,6},{6,7},{7,4},{8,9},{9,10},{10,1... | collective-permute-start | bytes 18874376 | tf_op jit(solution)/shard_map/ppermute | solution.py:95
  336.8 468.7 %collective-permute-start.6 = (bf16[512,6144]{1,0:T(8,128)(2,1)}, bf16[512,6144]{1,0:T(8,128)(2,1)}, u32[]{:S(2)}, u32[]{:S(2)}) collective-permute-start(bf16[512,6144]{1,0:T(8,128)(2,1)} %param.22), channel_id=1, source_target_pairs={{0,3},{1,0},{2,1},{3,2},{4,7},{5,4},{6,5},{7,6},{8,11},{9,8},{10,9... | collective-permute-start | bytes 18874376 | tf_op jit(solution)/shard_map/ppermute | solution.py:97
  339.7 439.1 %copy-start.50 = (f32[128]{0:T(128)}, f32[128]{0:T(128)S(1)}, u32[]{:S(2)}) copy-start(f32[128]{0:T(128)S(1)} %convert_element_type.205) | copy-start | bytes 1540
  892.6 288.0 %copy-start.11 = (f32[256,2048]{1,0:T(8,128)}, f32[256,2048]{1,0:T(8,128)S(1)}, u32[]{:S(2)}) copy-start(f32[256,2048]{1,0:T(8,128)S(1)} %get-tuple-element.513) | copy-start | bytes 6291460
  892.9 236.9 %copy-start.18 = (bf16[256,2048]{1,0:T(8,128)(2,1)}, bf16[256,2048]{1,0:T(8,128)(2,1)S(1)}, u32[]{:S(2)}) copy-start(bf16[256,2048]{1,0:T(8,128)(2,1)S(1)} %multiply_convert_fusion.3) | copy-start | bytes 3145732
  1203.1 328.4 %copy-start.31 = (f32[256,64]{0,1:T(8,128)S(1)}, f32[256,64]{0,1:T(8,128)}, u32[]{:S(2)}) copy-start(f32[256,64]{0,1:T(8,128)} %copy-done.30) | copy-start | bytes 196612
  1203.1 328.4 %copy-start.33 = (f32[256,64]{0,1:T(8,128)S(1)}, f32[256,64]{0,1:T(8,128)}, u32[]{:S(2)}) copy-start(f32[256,64]{0,1:T(8,128)} %copy-done.32) | copy-start | bytes 196612
  1203.1 329.9 %copy-start.41 = (f32[256,8]{0,1:T(8,128)S(1)}, f32[256,8]{0,1:T(8,128)}, u32[]{:S(2)}) copy-start(f32[256,8]{0,1:T(8,128)} %copy-done.40) | copy-start | bytes 24580
  1203.1 329.9 %copy-start.49 = (f32[128]{0:T(128)S(1)}, f32[128]{0:T(128)}, u32[]{:S(2)}) copy-start(f32[128]{0:T(128)} %copy-done.48) | copy-start | bytes 1540
  1216.8 10.7 collective-permute-start.2
  1219.0 14.2 collective-permute-start.3
  1220.4 18.3 collective-permute-start
  1220.6 23.8 collective-permute-start.1
  1257.8 10.7 collective-permute-start.2
  1260.0 14.2 collective-permute-start.3
  1260.0 19.8 collective-permute-start
  1260.0 25.4 collective-permute-start.1
  1298.8 10.7 collective-permute-start.2
  1301.0 14.2 collective-permute-start.3
  1301.0 19.8 collective-permute-start
  1301.0 25.4 collective-permute-start.1
  1339.8 10.7 collective-permute-start.2
  1342.0 14.2 collective-permute-start.3
  1342.0 19.8 collective-permute-start
  1342.0 25.4 collective-permute-start.1
  1380.9 10.7 collective-permute-start.2
  1383.0 14.2 collective-permute-start.3
  1383.0 19.8 collective-permute-start
  1383.0 25.4 collective-permute-start.1
  1421.9 10.7 collective-permute-start.2
  1424.1 14.2 collective-permute-start.3
  1424.1 19.8 collective-permute-start
  1424.1 25.4 collective-permute-start.1
  1462.9 10.7 collective-permute-start.2
  1465.1 14.2 collective-permute-start.3
  1465.1 19.8 collective-permute-start
  1465.1 25.4 collective-permute-start.1
  1503.9 10.7 collective-permute-start.2
  1506.1 14.2 collective-permute-start.3
  1506.1 19.8 collective-permute-start
  1506.1 25.4 collective-permute-start.1
  1572.2 848.5 %reduce-scatter.7.cloned.1.call-start = ((), (), s32[]{:S(2)}) async-start(), calls=%async_computation.11 | async-start | bytes 94371840
  1667.7 1247.9 %all-reduce.8.cloned.1.call-start = ((), (), s32[]{:S(2)}) async-start(), calls=%async_computation.12 | async-start | bytes 50331648 | tf_op jit(solution)/shard_map/psum | solution.py:324
  (79 other events, 370.9 us)
Sparse Core Ops, SparseCore 0:
  9.9 55.3 all-gather.10
  67.2 52.6 all-gather.14
  121.7 152.0 all-gather.18
  275.2 46.2 all-gather.12
  323.5 46.5 all-gather.16
  371.8 154.1 all-gather.20
  527.8 358.7 all-gather.22
  888.5 227.5 all-gather.24
  1572.3 219.1 reduce-scatter.4
  1794.7 625.8 reduce-scatter.6
  2423.3 492.2 all-reduce.7
